TPU v7x, 32 devices: a whole 2x2x4 slice. The times are simulated.
32 devices in a mesh: dp: 4 (over x, core), fsdp: 2 (over y), enc: 4 (over z).
Axes of the slice: x: 2, y: 2, z: 4, core: 2. Of those that a mesh axis runs over, the one named last changes fastest.
Arguments:
- hidden: bfloat16 [8192, 8192], P(('dp', 'fsdp', 'enc')), may hold values from -40 to 40
- residual_gradient: bfloat16 [8192, 8192], P(('dp', 'fsdp', 'enc')), may hold values from -3 to 3
- value_output_gradient: bfloat16 [8192, 1024], P(('dp', 'fsdp', 'enc')), may hold values from -6 to 6
- attention_norm_gain: float32 [8192], replicated, may hold values from 0.1 to 1.9
- value_frozen_weight: bfloat16 [8192, 1024], P('fsdp'), may hold values from -0.0625 to 0.0625
- value_down_factor: bfloat16 [8192, 16], replicated, may hold values from -0.0625 to 0.0625
- value_up_factor: bfloat16 [16, 1024], replicated, may hold values from -0.29882812 to 0.29882812
- merger_frozen_weight: bfloat16 [5120, 8192], P(None, ('fsdp', 'enc')), may hold values from -0.078125 to 0.078125
- merger_down_factor: bfloat16 [5120, 16], replicated, may hold values from -0.078125 to 0.078125
- merger_up_factor: bfloat16 [16, 8192], P(None, ('fsdp', 'enc')), may hold values from -0.29882812 to 0.29882812
- merger_saved_preactivation: bfloat16 [1024, 5120], P(('dp', 'fsdp', 'enc')), may hold values from -5 to 5
- image_token_counts: int32 [32], P('dp'), may hold values from 8 to 16, as said below
- image_encoder_owner: int32 [32], P('dp'), may hold values from 0 to 7, as said below
- image_first_rows: int32 [32], P(('dp', 'fsdp', 'enc')), may hold values from 0 to 255, as said below
Outputs:
- layer_input_gradient: bfloat16 [8192, 8192], P(('dp', 'fsdp', 'enc'))
- preactivation_gradient: bfloat16 [1024, 5120], P(('dp', 'fsdp', 'enc'))
- value_down_gradient: float32 [8192, 16], replicated
- value_up_gradient: float32 [16, 1024], replicated
- merger_down_gradient: float32 [5120, 16], replicated
- merger_up_gradient: float32 [16, 8192], P(None, ('fsdp', 'enc'))
Inputs may be any that keep to these rules, and one draw needn't show every extreme that they name: `image_token_counts`: within each data replica some encoder device owns exactly 2 images, all of 16 visual tokens, so its rows fill all 32; no other device owns more than 2 images. `image_encoder_owner`: encoder devices are numbered within the data replica in mesh order. `image_first_rows`: images of one device lie inside its 256 rows in increasing order and don't intersect.
All inputs are finite; a program needn't handle non-finite values.
Results may differ from a plain program's by a relative error of at most 0.0085.
Values may be sent and summed in bfloat16 or wider, within the bound.
No kernel may reach another device: no remote copies, remote signals or barrier semaphores. Data moves between devices by JAX's collectives and lax.ppermute only.
A program may use at most 192 MiB of HBM per device.

v0:
```python
import jax
import jax.numpy as jnp
from jax import lax
from jax.sharding import PartitionSpec as P

MAXIMG = 16
adapter_scale = 2.0
norm_eps = 1e-06


def gelu_parts(preact):
    normal_cdf = 0.5 * (1.0 + lax.erf(preact * 0.7071067811865476))
    normal_pdf = jnp.exp(-0.5 * preact * preact) * 0.3989422804014327
    return (normal_cdf, normal_pdf)


def owner_layout(image_token_counts, image_encoder_owner, owner_count, owner_room, slot_len):
    total_images = image_token_counts.shape[0]
    image_ids = jnp.arange(total_images)
    same_owner = image_encoder_owner[:, None] == image_encoder_owner[None, :]
    earlier = image_ids[None, :] < image_ids[:, None]
    starts = jnp.sum(jnp.where(same_owner & earlier, image_token_counts[None, :], 0), axis=1)
    row_index = jnp.arange(owner_count * owner_room)
    row_owner = row_index // owner_room
    row_place = row_index % owner_room
    matches = (
        (row_owner[:, None] == image_encoder_owner[None, :])
        & (row_place[:, None] >= starts[None, :])
        & (row_place[:, None] < (starts + image_token_counts)[None, :])
    )
    source = jnp.sum(
        jnp.where(matches, image_ids[None, :] * slot_len + row_place[:, None] - starts[None, :], 0),
        axis=1,
    )
    valid_rows = jnp.any(matches, axis=1)
    return (source, valid_rows)


def take_slots(layer_input_gradient, counts_in, offsets_in):
    padded = jnp.concatenate(
        [
            layer_input_gradient,
            jnp.zeros((MAXIMG, layer_input_gradient.shape[1]), layer_input_gradient.dtype),
        ],
        axis=0,
    )
    window = lax.dynamic_slice_in_dim(padded, offsets_in[0], MAXIMG, 0)
    inside = jnp.arange(MAXIMG) < counts_in[0]
    pieces = jnp.where(inside[:, None], window, jnp.zeros_like(window))
    return pieces


def decoder_layer_block(
    incoming_rows,
    residual_input,
    value_incoming,
    attention_norm_gain,
    passed_gradient,
    value_down_factor,
    value_up_factor,
):
    values = incoming_rows.astype(jnp.float32)
    inverse = lax.rsqrt(jnp.mean(values * values, axis=1, keepdims=True) + norm_eps)
    normalized_input = (values * inverse * attention_norm_gain).astype(jnp.bfloat16)
    value_low_product = jnp.dot(
        value_incoming, value_up_factor.T, preferred_element_type=jnp.float32
    ).astype(jnp.bfloat16)
    normalized_gradient = passed_gradient.astype(jnp.float32) + adapter_scale * jnp.dot(
        value_low_product, value_down_factor.T, preferred_element_type=jnp.float32
    )
    gained = attention_norm_gain * normalized_gradient
    layer_input_gradient = (
        residual_input.astype(jnp.float32)
        + inverse * gained
        - values * inverse**3 * jnp.mean(values * gained, axis=1, keepdims=True)
    ).astype(jnp.bfloat16)
    projected_rows = jnp.dot(
        normalized_input, value_down_factor, preferred_element_type=jnp.float32
    ).astype(jnp.bfloat16)
    up_term = lax.dot_general(
        projected_rows, value_incoming, (((0,), (0,)), ((), ())), preferred_element_type=jnp.float32
    )
    down_term = lax.dot_general(
        normalized_input,
        value_low_product,
        (((0,), (0,)), ((), ())),
        preferred_element_type=jnp.float32,
    )
    return (layer_input_gradient, down_term, up_term)


def body(
    hidden,
    residual_gradient,
    value_output_gradient,
    attention_norm_gain,
    value_frozen_weight,
    value_down_factor,
    value_up_factor,
    merger_frozen_weight,
    merger_down_factor,
    merger_up_factor,
    merger_saved_preactivation,
    image_token_counts,
    image_encoder_owner,
    image_first_rows,
):
    device_total = lax.axis_size("dp") * lax.axis_size("fsdp") * lax.axis_size("enc")
    gradient_scale = 256.0 / (hidden.shape[0] * device_total)
    scale_factor = gradient_scale * adapter_scale
    owner_count = lax.axis_size("fsdp") * lax.axis_size("enc")
    owner_room = merger_saved_preactivation.shape[0]
    preact = merger_saved_preactivation.astype(jnp.float32)
    normal_cdf, normal_pdf = gelu_parts(preact)
    activation = (preact * normal_cdf).astype(jnp.bfloat16)
    act_low = jnp.dot(activation, merger_down_factor, preferred_element_type=jnp.float32).astype(
        jnp.bfloat16
    )
    all_low = lax.all_gather(act_low, ("fsdp", "enc"), axis=0, tiled=True)
    columns = lax.dot_general(
        lax.all_gather(value_output_gradient, "fsdp", axis=0, tiled=True),
        value_frozen_weight,
        (((1,), (1,)), ((), ())),
        preferred_element_type=jnp.float32,
    ).astype(jnp.bfloat16)
    passed_gradient = lax.all_to_all(columns, "fsdp", split_axis=0, concat_axis=1, tiled=True)
    layer_input_gradient, down_term, up_term = decoder_layer_block(
        hidden,
        residual_gradient,
        value_output_gradient,
        attention_norm_gain,
        passed_gradient,
        value_down_factor,
        value_up_factor,
    )
    member = lax.axis_index(("fsdp", "enc"))
    local_images = image_first_rows.shape[0]
    local_counts = lax.dynamic_slice_in_dim(
        image_token_counts, member * local_images, local_images, 0
    )
    slots_out = take_slots(layer_input_gradient, local_counts, image_first_rows)
    received = lax.all_to_all(slots_out, ("fsdp", "enc"), split_axis=1, concat_axis=0, tiled=True)
    source, valid_rows = owner_layout(
        image_token_counts, image_encoder_owner, owner_count, owner_room, MAXIMG
    )
    visual_tokens = jnp.where(
        valid_rows[:, None], jnp.take(received, source, axis=0), jnp.zeros((), received.dtype)
    )
    value_partial_sum = lax.dot_general(
        visual_tokens,
        merger_frozen_weight,
        (((1,), (1,)), ((), ())),
        preferred_element_type=jnp.float32,
    )
    low_part = lax.dot_general(
        visual_tokens,
        merger_up_factor,
        (((1,), (1,)), ((), ())),
        preferred_element_type=jnp.float32,
    )
    value_partial_sum = value_partial_sum + adapter_scale * jnp.dot(
        low_part, merger_down_factor.astype(jnp.float32).T, precision=lax.Precision.HIGHEST
    )
    combined_gradient, low_sum = (
        lax.psum_scatter(value_partial_sum, ("fsdp", "enc"), scatter_dimension=0, tiled=True),
        lax.psum_scatter(low_part, ("fsdp", "enc"), scatter_dimension=0, tiled=True),
    )
    preactivation_gradient = (combined_gradient * (normal_cdf + preact * normal_pdf)).astype(
        jnp.bfloat16
    )
    term_a2 = lax.dot_general(
        activation,
        low_sum.astype(jnp.bfloat16),
        (((0,), (0,)), ((), ())),
        preferred_element_type=jnp.float32,
    )
    term_b2 = lax.dot_general(
        all_low, visual_tokens, (((0,), (0,)), ((), ())), preferred_element_type=jnp.float32
    )
    merger_up_gradient = lax.psum(scale_factor * term_b2, "dp")
    value_down_gradient, value_up_gradient, merger_down_gradient = lax.psum(
        (scale_factor * down_term, scale_factor * up_term, scale_factor * term_a2),
        ("dp", "fsdp", "enc"),
    )
    return (
        layer_input_gradient,
        preactivation_gradient,
        value_down_gradient,
        value_up_gradient,
        merger_down_gradient,
        merger_up_gradient,
    )


def solution(mesh):
    placed = (
        P(("dp", "fsdp", "enc"), None),
        P(("dp", "fsdp", "enc"), None),
        P(("dp", "fsdp", "enc"), None),
        P(),
        P("fsdp", None),
        P(),
        P(),
        P(None, ("fsdp", "enc")),
        P(),
        P(None, ("fsdp", "enc")),
        P(("dp", "fsdp", "enc"), None),
        P("dp"),
        P("dp"),
        P(("dp", "fsdp", "enc")),
    )
    return jax.shard_map(
        body,
        mesh=mesh,
        in_specs=placed,
        out_specs=(
            P(("dp", "fsdp", "enc"), None),
            P(("dp", "fsdp", "enc"), None),
            P(),
            P(),
            P(),
            P(None, ("fsdp", "enc")),
        ),
        check_vma=False,
    )
```

profile of v0, /device:TPU:0, one launch (start us, length us, event | category | flops | bytes accessed | tf_op | source)
XLA Modules:
  0.0 520.8 jit_solution(2232127266080886779)
XLA Ops:
  7.2 0.7 all-gather.3.cloned.1.call-update
  7.9 25.7 %all-gather.3.cloned.1.call-done = bf16[512,1024]{1,0:T(8,128)(2,1)} async-done(((bf16[256,1024]{1,0:T(8,128)(2,1)}), bf16[512,1024]{1,0:T(8,128)(2,1)}) %all-gather.3.cloned.1.call-update) | async-done | bytes 1048592 | tf_op jit(solution)/shard_map/all_gather | solution.py:121
  33.6 10.3 %convolution_convert_fusion = bf16[512,4096]{1,0:T(8,128)(2,1)} fusion(bf16[512,1024]{1,0:T(8,128)(2,1)} %all-gather.3.cloned.1.call-done, bf16[4096,1024]{1,0:T(8,128)(2,1)} %param.18), kind=kOutput, calls=%fused_computation.19 | convolution fusion | flops 4297064448 | bytes 13631488 | tf_op jit(solution)/shard_map/dot_general | solution.py:120
  43.9 5.7 %all-to-all-start = ((bf16[2,256,4096]{2,1,0:T(8,128)(2,1)}), bf16[2,256,4096]{2,1,0:T(8,128)(2,1)}, u32[]{:S(2)}, u32[]{:S(2)}) async-start(bf16[2,256,4096]{2,1,0:T(8,128)(2,1)} %bitcast.45), calls=%async_computation | async-start | bytes 8388608 | tf_op jit(solution)/shard_map/all_to_all | solution.py:126
  50.3 0.6 dynamic_slice.6
  50.9 0.2 select_reduce_fusion.1
  51.1 0.7 iota_compare_fusion.1
  51.7 0.1 select_reduce_fusion
  51.9 0.2 convolution_convert_fusion.1
  52.1 45.0 %all-to-all-done = bf16[2,256,4096]{2,1,0:T(8,128)(2,1)} async-done(((bf16[2,256,4096]{2,1,0:T(8,128)(2,1)}), bf16[2,256,4096]{2,1,0:T(8,128)(2,1)}, u32[]{:S(2)}, u32[]{:S(2)}) %all-to-all-start) | async-done | bytes 4194336 | tf_op jit(solution)/shard_map/all_to_all | solution.py:126
  97.1 3.3 convert_bitcast_fusion
  100.4 1.0 copy.34
  101.4 1.2 copy-done.1
  102.6 2.9 fusion.2
  105.5 3.5 fusion.5
  109.0 2.0 copy-done.2
  111.0 0.1 fusion.28
  111.2 0.7 copy.36
  111.9 4.6 all-to-all-start.1
  116.5 0.2 reduce-scatter.7.cloned.1.call-start
  116.7 0.1 fusion.33
  116.8 8.6 %all-to-all-done.1 = bf16[16,8,1024]{2,0,1:T(8,128)(2,1)S(1)} async-done(((bf16[16,8,1024]{2,0,1:T(8,128)(2,1)}), bf16[16,8,1024]{2,0,1:T(8,128)(2,1)S(1)}, u32[]{:S(2)}, u32[]{:S(2)}) %all-to-all-start.1) | async-done | bytes 262176 | tf_op jit(solution)/shard_map/all_to_all | solution.py:142
  125.4 1.2 gather_fusion
  126.6 0.1 select_select_fusion
  126.8 0.2 fusion.38
  127.0 12.6 %fusion.37 = f32[256,5120]{1,0:T(8,128)} fusion(bf16[256,1024]{1,0:T(8,128)(2,1)S(1)} %select_select_fusion, bf16[5120,1024]{1,0:T(8,128)(2,1)} %param.21), kind=kOutput, calls=%fused_computation.69 | convolution fusion | flops 2684354560 | bytes 16252928 | tf_op jit(solution)/shard_map/dot_general | solution.py:149
  139.6 0.8 copy.31
  140.4 0.0 reduce-scatter.5.cloned.1.call-start
  140.5 7.2 %fusion.9 = f32[256,5120]{1,0:T(8,128)} fusion(f32[256,5120]{1,0:T(8,128)} %fusion.37, f32[256,16]{0,1:T(8,128)S(1)} %fusion.38, bf16[5120,16]{0,1:T(8,128)(2,1)S(1)} %copy-done.6), kind=kOutput, calls=%fused_computation.18 | convolution fusion | flops 254279680 | bytes 10665984 | tf_op jit(solution)/shard_map/dot_general | solution.py:161
  147.7 0.0 all-reduce.5.cloned.1.call-start
  147.7 4.2 convolution_multiply_fusion.1
  151.9 4.4 convolution_multiply_fusion.5
  156.3 43.3 %reduce-scatter.7.cloned.1.call-done = f32[32,16]{1,0:T(8,128)} async-done(((f32[256,16]{1,0:T(8,128)}), f32[32,16]{1,0:T(8,128)}) %reduce-scatter.7.cloned.1.call-update) | async-done | bytes 2064
  199.6 0.8 copy.32
  200.4 104.9 %reduce-scatter.5.cloned.1.call-done = f32[32,5120]{1,0:T(8,128)} async-done(((f32[256,5120]{1,0:T(8,128)}), f32[32,5120]{1,0:T(8,128)}) %reduce-scatter.5.cloned.1.call-update) | async-done | bytes 655376 | tf_op jit(solution)/shard_map/reduce_scatter | solution.py:165
  305.3 2.1 fusion.26
  307.4 0.2 fusion.18
  307.6 30.6 %all-gather = bf16[8,32,16]{1,2,0:T(8,128)(2,1)S(1)} all-gather(bf16[1,32,16]{1,2,0:T(8,128)(2,1)S(1)} %fusion.18), channel_id=1, replica_groups=mesh['dp'=4,'fsdp'=2,'enc'=4] {'fsdp','enc'}, dimensions={0}, use_global_device_ids=true | all-gather | bytes 9216 | tf_op jit(solution)/shard_map/all_gather | solution.py:119
  338.2 0.1 reshape.104
  338.3 0.8 convolution_multiply_fusion.4
  339.2 0.0 all-reduce.7.cloned.1.call-start
  339.2 0.9 convolution_multiply_fusion.3
  340.2 30.3 %all-reduce.5.cloned.1.call-done = f32[16,1024]{1,0:T(8,128)} async-done(((f32[16,1024]{1,0:T(8,128)}), f32[16,1024]{1,0:T(8,128)}) %all-reduce.5.cloned.1.call-update) | async-done | bytes 65552 | tf_op jit(solution)/shard_map/psum | solution.py:180
  370.5 137.3 %all-reduce.7.cloned.1.call-done = (f32[8192,16]{0,1:T(8,128)}, f32[16,1024]{1,0:T(8,128)}, f32[5120,16]{0,1:T(8,128)}) async-done(((f32[8192,16]{0,1:T(8,128)}, f32[16,1024]{1,0:T(8,128)}, f32[5120,16]{0,1:T(8,128)}), (f32[8192,16]{0,1:T(8,128)}, f32[16,1024]{1,0:T(8,128)}, f32[5120,16]{0,1:T(8,128)})) %all-reduce.7.cloned.1.call-update) | async-done | bytes 917520 | tf_op jit(solution)/shard_map/psum | solution.py:181
  507.7 1.9 copy.42
  509.6 1.5 copy.43
  511.1 1.7 copy.44
  512.8 1.5 copy.45
  (35 shorter events, 0.2 us)
Async XLA Ops:
  7.2 94.2 %copy-start = (bf16[8192,16]{0,1:T(8,128)(2,1)S(1)}, bf16[8192,16]{0,1:T(8,128)(2,1)}, u32[]{:S(2)}) copy-start(bf16[8192,16]{0,1:T(8,128)(2,1)} %param.19) | copy-start | bytes 786436
  7.2 26.4 %all-gather.3.cloned.1.call-start = ((), (), s32[]{:S(2)}) async-start(), calls=%async_computation.4 | async-start | bytes 1572864 | tf_op jit(solution)/shard_map/all_gather | solution.py:121
  43.8 6.4 %copy-start.11 = (s32[8]{0:T(128)S(1)}, s32[8]{0:T(128)}, u32[]{:S(2)}) copy-start(s32[8]{0:T(128)} %param.25) | copy-start | bytes 100
  43.9 7.0 %copy-start.10 = (s32[8]{0:T(128)S(1)}, s32[8]{0:T(128)}, u32[]{:S(2)}) copy-start(s32[8]{0:T(128)} %param.26) | copy-start | bytes 100
  43.9 8.0 %copy-start.5 = (bf16[256,1024]{1,0:T(8,128)(2,1)S(1)}, bf16[256,1024]{1,0:T(8,128)(2,1)}, u32[]{:S(2)}) copy-start(bf16[256,1024]{1,0:T(8,128)(2,1)} %param.16) | copy-start | bytes 1572868
  43.9 8.0 %copy-start.8 = (bf16[16,1024]{1,0:T(8,128)(2,1)S(1)}, bf16[16,1024]{1,0:T(8,128)(2,1)}, u32[]{:S(2)}) copy-start(bf16[16,1024]{1,0:T(8,128)(2,1)} %param.20) | copy-start | bytes 98308
  43.9 53.3 %all-to-all-start = ((bf16[2,256,4096]{2,1,0:T(8,128)(2,1)}), bf16[2,256,4096]{2,1,0:T(8,128)(2,1)}, u32[]{:S(2)}, u32[]{:S(2)}) async-start(bf16[2,256,4096]{2,1,0:T(8,128)(2,1)} %bitcast.45), calls=%async_computation | async-start | bytes 8388608 | tf_op jit(solution)/shard_map/all_to_all | solution.py:126
  100.4 2.2 copy-start.1
  100.4 2.2 copy-start.7
  102.6 2.9 copy-start.3
  109.0 2.0 copy-start.2
  111.0 15.7 %copy-start.9 = (bf16[16,1024]{1,0:T(8,128)(2,1)S(1)}, bf16[16,1024]{1,0:T(8,128)(2,1)}, u32[]{:S(2)}) copy-start(bf16[16,1024]{1,0:T(8,128)(2,1)} %param.23) | copy-start | bytes 98308
  111.9 13.6 %all-to-all-start.1 = ((bf16[16,8,1024]{2,0,1:T(8,128)(2,1)}), bf16[16,8,1024]{2,0,1:T(8,128)(2,1)S(1)}, u32[]{:S(2)}, u32[]{:S(2)}) async-start(bf16[16,8,1024]{2,0,1:T(8,128)(2,1)} %bitcast.39), calls=%async_computation.1 | async-start | bytes 524288 | tf_op jit(solution)/shard_map/all_to_all | solution.py:142
  116.5 83.1 %reduce-scatter.7.cloned.1.call-start = ((), (), s32[]{:S(2)}) async-start(), calls=%async_computation.7 | async-start | bytes 147456
  127.0 13.4 %copy-start.6 = (bf16[5120,16]{0,1:T(8,128)(2,1)S(1)}, bf16[5120,16]{0,1:T(8,128)(2,1)}, u32[]{:S(2)}) copy-start(bf16[5120,16]{0,1:T(8,128)(2,1)} %param.22) | copy-start | bytes 491524
  140.4 164.9 %reduce-scatter.5.cloned.1.call-start = ((), (), s32[]{:S(2)}) async-start(), calls=%async_computation.5 | async-start | bytes 5898240 | tf_op jit(solution)/shard_map/reduce_scatter | solution.py:165
  147.7 157.6 %copy-start.4 = (bf16[32,5120]{1,0:T(8,128)(2,1)S(1)}, bf16[32,5120]{1,0:T(8,128)(2,1)}, u32[]{:S(2)}) copy-start(bf16[32,5120]{1,0:T(8,128)(2,1)} %param.24) | copy-start | bytes 983044
  147.7 222.8 %all-reduce.5.cloned.1.call-start = ((), (), s32[]{:S(2)}) async-start(), calls=%async_computation.6 | async-start | bytes 131072 | tf_op jit(solution)/shard_map/psum | solution.py:180
  339.2 168.6 %all-reduce.7.cloned.1.call-start = ((), (), s32[]{:S(2)}) async-start(), calls=%async_computation.8 | async-start | bytes 1835008 | tf_op jit(solution)/shard_map/psum | solution.py:181
Sparse Core Ops, SparseCore 0:
  9.5 23.9 all-gather.2
  140.5 59.0 reduce-scatter.6
  203.2 102.0 reduce-scatter.4
  339.3 31.1 all-reduce.4
  376.4 131.3 all-reduce.6
where the time goes:
time: 522 us; the launch traced here: 521 us
  waiting for transfers between devices  396 us (76%)
  matrix products  44 us (8%)
  blocking collectives  30.6 us (6%)
  local copies, waits for them, and re-layouts  14.9 us (3%)
  between operations  14.6 us (3%)
  starting transfers between devices  10.7 us (2%)
  other arithmetic  10.2 us (2%)
    psum x1, waiting for transfers between devices, body(): lax.psum((scale_factor * down_term, scale_factor * up_term, scale_factor...  137 us
    reduce_scatter x1, waiting for transfers between devices, body(): lax.psum_scatter(value_partial_sum, ('fsdp', 'enc'), scatter_dimension=0,...  105 us
    all_to_all x1, waiting for transfers between devices, body(): lax.all_to_all(columns, 'fsdp', split_axis=0, concat_axis=1, tiled=True)  45 us
    unnamed x6, waiting for transfers between devices  44.1 us
    all_gather x1, blocking collectives, body(): all_low = lax.all_gather(act_low, ('fsdp', 'enc'), axis=0, tiled=True)  30.6 us
    psum x1, waiting for transfers between devices, body(): merger_up_gradient = lax.psum(scale_factor * term_b2, 'dp')  30.3 us
    all_gather x1, waiting for transfers between devices, body(): lax.all_gather(value_output_gradient, 'fsdp', axis=0, tiled=True)  25.7 us
    dot_general x1, matrix products, body(): lax.dot_general(visual_tokens, merger_frozen_weight, (((1,), (1,)), ((),...  12.6 us
  transfers between devices with their start and end apart: 7, of which 7 were waited for; matrix products, arithmetic and copies ran while one was open for 4% of the time, Pallas kernels for 0%

commit v1 on v0

--- a/solution.py
+++ b/solution.py
@@ -177,7 +177,7 @@
     term_b2 = lax.dot_general(
         all_low, visual_tokens, (((0,), (0,)), ((), ())), preferred_element_type=jnp.float32
     )
-    merger_up_gradient = lax.psum(scale_factor * term_b2, "dp")
+    merger_up_gradient = jnp.sum(lax.all_gather(scale_factor * term_b2, "dp"), axis=0)
     value_down_gradient, value_up_gradient, merger_down_gradient = lax.psum(
         (scale_factor * down_term, scale_factor * up_term, scale_factor * term_a2),
         ("dp", "fsdp", "enc"),

time: 522 us -> 454 us (0.87)
  waiting for transfers between devices: 396 us -> 325 us
  blocking collectives: 30.6 us -> 36.4 us
    psum x1, waiting for transfers between devices: 137 us -> 96.3 us  [body(): lax.psum((scale_factor * down_term, scale_factor * up_term, scale_factor...]
    psum x1 -> x0, waiting for transfers between devices: 30.3 us -> none  [body(): merger_up_gradient = lax.psum(scale_factor * term_b2, 'dp')]
    all_gather x0 -> x1, blocking collectives: none -> 5.77 us  [body(): lax.all_gather(scale_factor * term_b2, 'dp')]
    unnamed x31 -> x30, local copies, waits for them, and re-layouts: 11.4 us -> 9.92 us
    unnamed x6 -> x5, waiting for transfers between devices: 44.1 us -> 44.1 us
  transfers between devices with their start and end apart: 7 -> 6, of which waited for: 7 -> 6; matrix products, arithmetic and copies ran while one was open for 4% -> 4% of each run, Pallas kernels for 0% -> 0%
where the time goes in v1:
time: 454 us
  waiting for transfers between devices  325 us (72%)
  matrix products  43.3 us (10%)
  blocking collectives  36.4 us (8%)
  between operations  14.6 us (3%)
  local copies, waits for them, and re-layouts  13.4 us (3%)
  other arithmetic  10.8 us (2%)
  starting transfers between devices  10.7 us (2%)
    reduce_scatter x1, waiting for transfers between devices, body(): lax.psum_scatter(value_partial_sum, ('fsdp', 'enc'), scatter_dimension=0,...  105 us
    psum x1, waiting for transfers between devices, body(): lax.psum((scale_factor * down_term, scale_factor * up_term, scale_factor...  96.3 us
    all_to_all x1, waiting for transfers between devices, body(): lax.all_to_all(columns, 'fsdp', split_axis=0, concat_axis=1, tiled=True)  45 us
    unnamed x5, waiting for transfers between devices  44.1 us
    all_gather x1, blocking collectives, body(): all_low = lax.all_gather(act_low, ('fsdp', 'enc'), axis=0, tiled=True)  30.7 us
    all_gather x1, waiting for transfers between devices, body(): lax.all_gather(value_output_gradient, 'fsdp', axis=0, tiled=True)  25.7 us
    dot_general x1, matrix products, body(): lax.dot_general(visual_tokens, merger_frozen_weight, (((1,), (1,)), ((),...  12.6 us
    dot_general x1, matrix products, body(): lax.dot_general(lax.all_gather(value_output_gradient, 'fsdp', axis=0, til...  10.3 us
  transfers between devices with their start and end apart: 6, of which 6 were waited for; matrix products, arithmetic and copies ran while one was open for 4% of the time, Pallas kernels for 0%

profile of v1, /device:TPU:0, one launch (start us, length us, event | category | flops | bytes accessed | tf_op | source)
XLA Modules:
  0.0 453.8 jit_solution(10912520534768746710)
XLA Ops:
  7.2 0.0 all-gather.4.cloned.1.call-start
  7.2 0.7 all-gather.4.cloned.1.call-update
  7.9 25.7 %all-gather.4.cloned.1.call-done = bf16[512,1024]{1,0:T(8,128)(2,1)} async-done(((bf16[256,1024]{1,0:T(8,128)(2,1)}), bf16[512,1024]{1,0:T(8,128)(2,1)}) %all-gather.4.cloned.1.call-update) | async-done | bytes 1048592 | tf_op jit(solution)/shard_map/all_gather | solution.py:121
  33.6 10.3 %convolution_convert_fusion = bf16[512,4096]{1,0:T(8,128)(2,1)} fusion(bf16[512,1024]{1,0:T(8,128)(2,1)} %all-gather.4.cloned.1.call-done, bf16[4096,1024]{1,0:T(8,128)(2,1)} %param.18), kind=kOutput, calls=%fused_computation.19 | convolution fusion | flops 4297064448 | bytes 13631488 | tf_op jit(solution)/shard_map/dot_general | solution.py:120
  43.9 5.8 %all-to-all-start = ((bf16[2,256,4096]{2,1,0:T(8,128)(2,1)}), bf16[2,256,4096]{2,1,0:T(8,128)(2,1)}, u32[]{:S(2)}, u32[]{:S(2)}) async-start(bf16[2,256,4096]{2,1,0:T(8,128)(2,1)} %bitcast.46), calls=%async_computation | async-start | bytes 8388608 | tf_op jit(solution)/shard_map/all_to_all | solution.py:126
  50.3 0.6 dynamic_slice.6
  50.9 0.2 select_reduce_fusion.1
  51.1 0.7 iota_compare_fusion.1
  51.8 0.1 select_reduce_fusion
  51.9 0.2 convolution_convert_fusion.1
  52.1 45.0 %all-to-all-done = bf16[2,256,4096]{2,1,0:T(8,128)(2,1)} async-done(((bf16[2,256,4096]{2,1,0:T(8,128)(2,1)}), bf16[2,256,4096]{2,1,0:T(8,128)(2,1)}, u32[]{:S(2)}, u32[]{:S(2)}) %all-to-all-start) | async-done | bytes 4194336 | tf_op jit(solution)/shard_map/all_to_all | solution.py:126
  97.1 3.3 convert_bitcast_fusion
  100.4 1.0 copy.34
  101.4 1.2 copy-done.1
  102.6 2.9 fusion.2
  105.5 3.5 fusion.5
  109.0 2.0 copy-done.2
  111.0 0.1 fusion.28
  111.2 0.7 copy.36
  111.9 4.6 %all-to-all-start.1 = ((bf16[16,8,1024]{2,0,1:T(8,128)(2,1)}), bf16[16,8,1024]{2,0,1:T(8,128)(2,1)S(1)}, u32[]{:S(2)}, u32[]{:S(2)}) async-start(bf16[16,8,1024]{2,0,1:T(8,128)(2,1)} %bitcast.40), calls=%async_computation.1 | async-start | bytes 524288 | tf_op jit(solution)/shard_map/all_to_all | solution.py:142
  116.5 0.2 reduce-scatter.7.cloned.1.call-start
  116.8 0.1 fusion.33
  116.9 8.6 %all-to-all-done.1 = bf16[16,8,1024]{2,0,1:T(8,128)(2,1)S(1)} async-done(((bf16[16,8,1024]{2,0,1:T(8,128)(2,1)}), bf16[16,8,1024]{2,0,1:T(8,128)(2,1)S(1)}, u32[]{:S(2)}, u32[]{:S(2)}) %all-to-all-start.1) | async-done | bytes 262176 | tf_op jit(solution)/shard_map/all_to_all | solution.py:142
  125.5 1.2 gather_fusion
  126.6 0.1 select_select_fusion
  126.8 0.2 fusion.38
  127.0 12.6 %fusion.37 = f32[256,5120]{1,0:T(8,128)} fusion(bf16[256,1024]{1,0:T(8,128)(2,1)S(1)} %select_select_fusion, bf16[5120,1024]{1,0:T(8,128)(2,1)} %param.21), kind=kOutput, calls=%fused_computation.69 | convolution fusion | flops 2684354560 | bytes 16252928 | tf_op jit(solution)/shard_map/dot_general | solution.py:149
  139.6 0.8 copy.31
  140.4 0.0 reduce-scatter.5.cloned.1.call-start
  140.5 7.2 %fusion.9 = f32[256,5120]{1,0:T(8,128)} fusion(f32[256,5120]{1,0:T(8,128)} %fusion.37, f32[256,16]{0,1:T(8,128)S(1)} %fusion.38, bf16[5120,16]{0,1:T(8,128)(2,1)S(1)} %copy-done.6), kind=kOutput, calls=%fused_computation.18 | convolution fusion | flops 254279680 | bytes 10665984 | tf_op jit(solution)/shard_map/dot_general | solution.py:161
  147.7 0.0 all-reduce.4.cloned.1.call-start
  147.7 4.2 convolution_multiply_fusion.1
  151.9 4.4 convolution_multiply_fusion.5
  156.3 43.4 %reduce-scatter.7.cloned.1.call-done = f32[32,16]{1,0:T(8,128)} async-done(((f32[256,16]{1,0:T(8,128)}), f32[32,16]{1,0:T(8,128)}) %reduce-scatter.7.cloned.1.call-update) | async-done | bytes 2064
  199.7 0.8 copy.32
  200.5 104.9 %reduce-scatter.5.cloned.1.call-done = f32[32,5120]{1,0:T(8,128)} async-done(((f32[256,5120]{1,0:T(8,128)}), f32[32,5120]{1,0:T(8,128)}) %reduce-scatter.5.cloned.1.call-update) | async-done | bytes 655376 | tf_op jit(solution)/shard_map/reduce_scatter | solution.py:165
  305.3 2.1 fusion.26
  307.4 0.9 convolution_multiply_fusion.3
  308.4 0.2 fusion.18
  308.6 30.7 %all-gather.1 = bf16[8,32,16]{1,2,0:T(8,128)(2,1)S(1)} all-gather(bf16[1,32,16]{1,2,0:T(8,128)(2,1)S(1)} %fusion.18), channel_id=1, replica_groups=mesh['dp'=4,'fsdp'=2,'enc'=4] {'fsdp','enc'}, dimensions={0}, use_global_device_ids=true | all-gather | bytes 9216 | tf_op jit(solution)/shard_map/all_gather | solution.py:119
  339.3 0.1 reshape.105
  339.4 0.2 convolution_multiply_fusion.4
  339.5 5.8 %all-gather = f32[64,1024]{1,0:T(8,128)S(1)} all-gather(f32[16,1024]{1,0:T(8,128)S(1)} %convolution_multiply_fusion.4), channel_id=2, replica_groups=mesh['dp'=4,'fsdp'=2,'enc'=4] {'dp'}, dimensions={0}, use_global_device_ids=true | all-gather | bytes 327680 | tf_op jit(solution)/shard_map/all_gather | solution.py:180
  345.3 0.6 reduce_sum.52
  345.9 96.3 %all-reduce.4.cloned.1.call-done = (f32[8192,16]{0,1:T(8,128)}, f32[16,1024]{1,0:T(8,128)}, f32[5120,16]{0,1:T(8,128)}) async-done(((f32[8192,16]{0,1:T(8,128)}, f32[16,1024]{1,0:T(8,128)}, f32[5120,16]{0,1:T(8,128)}), (f32[8192,16]{0,1:T(8,128)}, f32[16,1024]{1,0:T(8,128)}, f32[5120,16]{0,1:T(8,128)})) %all-reduce.4.cloned.1.call-update) | async-done | bytes 917520 | tf_op jit(solution)/shard_map/psum | solution.py:181
  442.2 1.9 copy.41
  444.1 1.5 copy.42
  445.5 1.7 copy.43
  (33 shorter events, 0.2 us)
Async XLA Ops:
  7.2 94.2 %copy-start = (bf16[8192,16]{0,1:T(8,128)(2,1)S(1)}, bf16[8192,16]{0,1:T(8,128)(2,1)}, u32[]{:S(2)}) copy-start(bf16[8192,16]{0,1:T(8,128)(2,1)} %param.19) | copy-start | bytes 786436
  7.2 26.4 %all-gather.4.cloned.1.call-start = ((), (), s32[]{:S(2)}) async-start(), calls=%async_computation.4 | async-start | bytes 1572864 | tf_op jit(solution)/shard_map/all_gather | solution.py:121
  43.8 6.4 %copy-start.11 = (s32[8]{0:T(128)S(1)}, s32[8]{0:T(128)}, u32[]{:S(2)}) copy-start(s32[8]{0:T(128)} %param.25) | copy-start | bytes 100
  43.8 7.0 %copy-start.10 = (s32[8]{0:T(128)S(1)}, s32[8]{0:T(128)}, u32[]{:S(2)}) copy-start(s32[8]{0:T(128)} %param.26) | copy-start | bytes 100
  43.8 8.0 %copy-start.5 = (bf16[256,1024]{1,0:T(8,128)(2,1)S(1)}, bf16[256,1024]{1,0:T(8,128)(2,1)}, u32[]{:S(2)}) copy-start(bf16[256,1024]{1,0:T(8,128)(2,1)} %param.16) | copy-start | bytes 1572868
  43.9 8.0 %copy-start.8 = (bf16[16,1024]{1,0:T(8,128)(2,1)S(1)}, bf16[16,1024]{1,0:T(8,128)(2,1)}, u32[]{:S(2)}) copy-start(bf16[16,1024]{1,0:T(8,128)(2,1)} %param.20) | copy-start | bytes 98308
  43.9 53.3 %all-to-all-start = ((bf16[2,256,4096]{2,1,0:T(8,128)(2,1)}), bf16[2,256,4096]{2,1,0:T(8,128)(2,1)}, u32[]{:S(2)}, u32[]{:S(2)}) async-start(bf16[2,256,4096]{2,1,0:T(8,128)(2,1)} %bitcast.46), calls=%async_computation | async-start | bytes 8388608 | tf_op jit(solution)/shard_map/all_to_all | solution.py:126
  100.4 2.2 copy-start.1
  100.4 2.2 copy-start.7
  102.6 2.9 copy-start.3
  109.0 2.0 copy-start.2
  111.0 15.7 %copy-start.9 = (bf16[16,1024]{1,0:T(8,128)(2,1)S(1)}, bf16[16,1024]{1,0:T(8,128)(2,1)}, u32[]{:S(2)}) copy-start(bf16[16,1024]{1,0:T(8,128)(2,1)} %param.23) | copy-start | bytes 98308
  111.9 13.6 %all-to-all-start.1 = ((bf16[16,8,1024]{2,0,1:T(8,128)(2,1)}), bf16[16,8,1024]{2,0,1:T(8,128)(2,1)S(1)}, u32[]{:S(2)}, u32[]{:S(2)}) async-start(bf16[16,8,1024]{2,0,1:T(8,128)(2,1)} %bitcast.40), calls=%async_computation.1 | async-start | bytes 524288 | tf_op jit(solution)/shard_map/all_to_all | solution.py:142
  116.5 83.2 %reduce-scatter.7.cloned.1.call-start = ((), (), s32[]{:S(2)}) async-start(), calls=%async_computation.6 | async-start | bytes 147456
  127.0 13.4 %copy-start.6 = (bf16[5120,16]{0,1:T(8,128)(2,1)S(1)}, bf16[5120,16]{0,1:T(8,128)(2,1)}, u32[]{:S(2)}) copy-start(bf16[5120,16]{0,1:T(8,128)(2,1)} %param.22) | copy-start | bytes 491524
  140.4 164.9 %reduce-scatter.5.cloned.1.call-start = ((), (), s32[]{:S(2)}) async-start(), calls=%async_computation.5 | async-start | bytes 5898240 | tf_op jit(solution)/shard_map/reduce_scatter | solution.py:165
  147.7 157.7 %copy-start.4 = (bf16[32,5120]{1,0:T(8,128)(2,1)S(1)}, bf16[32,5120]{1,0:T(8,128)(2,1)}, u32[]{:S(2)}) copy-start(bf16[32,5120]{1,0:T(8,128)(2,1)} %param.24) | copy-start | bytes 983044
  147.7 294.5 %all-reduce.4.cloned.1.call-start = ((), (), s32[]{:S(2)}) async-start(), calls=%async_computation.7 | async-start | bytes 1835008 | tf_op jit(solution)/shard_map/psum | solution.py:181
Sparse Core Ops, SparseCore 0:
  9.5 23.9 all-gather.3
  140.5 59.0 reduce-scatter.6
  203.3 102.0 reduce-scatter.4
  311.2 130.9 all-reduce.3
